TPU v7x, 32 devices: a whole 2x2x4 slice. The times are simulated.
32 devices in a mesh: event: 2 (over y), mesh: 16 (over z, x, core).
Axes of the slice: x: 2, y: 2, z: 4, core: 2. Of those that a mesh axis runs over, the one named last changes fastest.
Arguments:
- forward_before: float32 [2, 3, 128, 8, 128], P('event', None, 'mesh'), may hold values from -3 to 3
- forward_now: float32 [2, 3, 128, 8, 128], P('event', None, 'mesh'), may hold values from -3 to 3
- adjoint_after: float32 [2, 3, 128, 8, 128], P('event', None, 'mesh'), may hold values from -3 to 3
- adjoint_now: float32 [2, 3, 128, 8, 128], P('event', None, 'mesh'), may hold values from -3 to 3
- mass_density: float32 [125, 2048], P(None, 'mesh'), may hold values from 0.8 to 1.5
- lame_lambda: float32 [125, 2048], P(None, 'mesh'), may hold values from 0.3 to 1
- lame_mu: float32 [125, 2048], P(None, 'mesh'), may hold values from 0.3 to 1
- source_element: int32 [2], P('event'), may hold values from 0 to 2047
- source_offset: int32 [2, 3], P('event'), may hold values from 0 to 4
- source_force: float32 [2, 3, 3], P('event'), may hold values from -120 to 120
- receiver_element: int32 [2, 32], P('event'), may hold values from 0 to 2047
- receiver_offset: int32 [2, 32, 3], P('event'), may hold values from 0 to 4
- receiver_data: float32 [2, 3, 32, 3], P('event'), may hold values from -3 to 3
Outputs:
- forward_final: float32 [2, 3, 128, 8, 128], P('event', None, 'mesh')
- adjoint_final: float32 [2, 3, 128, 8, 128], P('event', None, 'mesh')
- kernels: float32 [2, 125, 2048], P(None, None, ('mesh', 'event'))
Inputs may be any that keep to these rules, and one draw needn't show every extreme that they name: `source_element`: element e lies at depth layer e // 64, row (e // 32) % 2, column e % 32. `source_offset`: offsets along depth, row, column; a point on the fixed bottom plane takes no force. `receiver_element`: element e lies at depth layer e // 64, row (e // 32) % 2, column e % 32; receivers may share points. `receiver_offset`: offsets along depth, row, column; a receiver on the fixed bottom plane records zero and takes no force.
All inputs are finite; a program needn't handle non-finite values.
Results may differ from a plain program's by a relative error of at most 0.0003.
Values sent between devices are 32-bit elements; how exact they have to be, the bound alone decides.
A program may use at most 192 MiB of HBM per device.

v0:
```python
import functools
import math

import jax
import jax.numpy as jnp
import numpy as np
from jax import lax
from jax.experimental import pallas as pl
from jax.experimental.pallas import tpu as pltpu
from jax.sharding import PartitionSpec as P

time_step = 0.04
adjoint_gain = 25.0
LANES = 128


def numpy_tables():
    gll_points = np.array([-1.0, -math.sqrt(3.0 / 7.0), 0.0, math.sqrt(3.0 / 7.0), 1.0])
    legendre = (35.0 * gll_points**4 - 30.0 * gll_points**2 + 3.0) / 8.0
    deriv_table = np.zeros((5, 5))
    for row_q in range(5):
        for col_k in range(5):
            if row_q != col_k:
                deriv_table[row_q, col_k] = legendre[row_q] / (
                    legendre[col_k] * (gll_points[row_q] - gll_points[col_k])
                )
    deriv_table[0, 0] = -5.0
    deriv_table[4, 4] = 5.0
    gll_weights = np.array([0.1, 49.0 / 90.0, 32.0 / 45.0, 49.0 / 90.0, 0.1])
    return (deriv_table, gll_weights)


DERIV, WEIGHTS = numpy_tables()


def constants():
    spread = np.zeros((4, LANES, 4, 4, 32), np.float32)
    for j in range(4):
        for ex in range(32):
            for c in range(4):
                spread[j, 4 * ex + c, c, j, ex] = 1.0
    spread = spread.reshape(512, 512)
    rows = np.zeros((5, 5, 8, 125), np.float32)
    cube = np.zeros((5, 5, 8, LANES), np.float32)
    for a in range(5):
        for b in range(5):
            for c in range(5):
                rows[a, c, b, (a * 5 + b) * 5 + c] = 1.0
                cube[a, c, b, :] = WEIGHTS[a] * WEIGHTS[b] * WEIGHTS[c]
    rows = rows.reshape(200, 125)
    dy = np.zeros((2, 5, 8, LANES), np.float32)
    for k in range(5):
        for b in range(5):
            dy[0, k, b, :] = DERIV[b, k]
            dy[1, k, b, :] = DERIV[k, b]
    dz = np.stack([DERIV, DERIV.T]).reshape(-1).astype(np.float32)
    bf = jnp.bfloat16
    return (
        jnp.asarray(spread, bf),
        jnp.asarray(np.ascontiguousarray(spread.T), bf),
        jnp.asarray(rows, bf),
        jnp.asarray(np.ascontiguousarray(rows.T), bf),
        jnp.asarray(cube),
        jnp.asarray(dy),
        jnp.asarray(dz),
    )


def split3(value):
    high = value.astype(jnp.bfloat16)
    rest = value - high.astype(jnp.float32)
    middle = rest.astype(jnp.bfloat16)
    low = (rest - middle.astype(jnp.float32)).astype(jnp.bfloat16)
    return (high, middle, low)


def dot(left, right):
    return jnp.dot(left, right, preferred_element_type=jnp.float32)


def move_right(values, table):
    high, middle, low = split3(values)
    return dot(high, table) + dot(middle, table) + dot(low, table)


def move_left(table, values):
    high, middle, low = split3(values)
    return dot(table, high) + dot(table, middle) + dot(table, low)


def roll_lane(value, shift):
    return pltpu.roll(value, shift % LANES, value.ndim - 1)


def lane_iota(ndim):
    return lax.broadcasted_iota(jnp.int32, (1,) * (ndim - 1) + (LANES,), ndim - 1)


def sub_iota(ndim):
    return lax.broadcasted_iota(jnp.int32, (1,) * (ndim - 2) + (8, LANES), ndim - 2)


def pick(mask, first, second):
    return jnp.where(jnp.broadcast_to(mask, first.shape), first, second)


def from_left(value):
    at_edge = lane_iota(value.ndim) % 32 == 0
    return pick(at_edge, roll_lane(value, -31), roll_lane(value, 1))


def from_right(value):
    at_edge = lane_iota(value.ndim) % 32 == 31
    return pick(at_edge, roll_lane(value, 31), roll_lane(value, -1))


def roll_sub(value):
    return pltpu.roll(value, 4, value.ndim - 2)


def assemble_xy(value):
    first = value[:, 0:1] + from_left(value[:, 4:5])
    value = jnp.concatenate([first, value[:, 1:4], from_right(first)], axis=1)
    swapped = roll_sub(value)
    other = pick(
        lane_iota(4) % 64 < 32, roll_lane(swapped, -32), roll_lane(swapped, 32)
    )
    return value + pick(sub_iota(4) % 4 == 0, other, jnp.zeros_like(other))


def kernel(
    n_mesh,
    n_event,
    steps,
    now_ref,
    before_ref,
    adj_ref,
    after_ref,
    rho_ref,
    lam_ref,
    mu_ref,
    src_ref,
    force_ref,
    rec_elem_ref,
    rec_off_ref,
    data_ref,
    spread_ref,
    gather_ref,
    rows_ref,
    rows_t_ref,
    cube_ref,
    dy_ref,
    dz_ref,
    final_f_ref,
    final_a_ref,
    out_ref,
    fields,
    stress,
    force,
    strains,
    ksum,
    clam,
    cmu,
    minv,
    halo_s,
    halo_r,
    up_s,
    up_r,
    down_s,
    down_r,
    ev_s,
    ev_r,
    s_up,
    r_up,
    s_down,
    r_down,
    s_ev,
    r_ev,
):
    me = lax.axis_index("mesh")
    event = lax.axis_index("event")
    has_up = me > 0
    has_down = me < n_mesh - 1

    barrier = pltpu.get_barrier_semaphore()

    @pl.when(has_up)
    def _():
        pl.semaphore_signal(barrier, inc=1, device_id={"mesh": me - 1})

    @pl.when(has_down)
    def _():
        pl.semaphore_signal(barrier, inc=1, device_id={"mesh": me + 1})

    for hop in range(1, n_event):
        pl.semaphore_signal(
            barrier, inc=1, device_id={"event": lax.rem(event + hop, n_event)}
        )

    inputs = (now_ref, before_ref, adj_ref, after_ref)
    for index, ref in enumerate(inputs):
        halo_s[index] = ref[0, :, 0]

    pl.semaphore_wait(
        barrier,
        jnp.where(has_up, 1, 0) + jnp.where(has_down, 1, 0) + (n_event - 1),
    )

    def up_copy(source, target, slot):
        return pltpu.make_async_remote_copy(
            src_ref=source, dst_ref=target, send_sem=s_up.at[slot],
            recv_sem=r_up.at[slot], device_id={"mesh": me - 1},
        )

    def down_copy(source, target, slot):
        return pltpu.make_async_remote_copy(
            src_ref=source, dst_ref=target, send_sem=s_down.at[slot],
            recv_sem=r_down.at[slot], device_id={"mesh": me + 1},
        )

    halo_slot = steps * 2 + 1

    @pl.when(has_up)
    def _():
        up_copy(halo_s, halo_r, halo_slot).start()

    @pl.when(jnp.logical_not(has_down))
    def _():
        halo_r[...] = jnp.zeros_like(halo_r)
        up_r[...] = jnp.zeros_like(up_r)

    @pl.when(jnp.logical_not(has_up))
    def _():
        down_r[...] = jnp.zeros_like(down_r)

    low_half = lane_iota(4) < 64

    def send_faces(top, bottom, slot):
        count = top.shape[0]
        for pair in range(2):
            c = 2 * pair
            up_s[slot, 0:count, pair] = pick(
                low_half, top[:, c : c + 1], roll_lane(top[:, c + 1 : c + 2], 64)
            )[:, 0]
            down_s[slot, 0:count, pair] = pick(
                low_half, roll_lane(bottom[:, c : c + 1], 64), bottom[:, c + 1 : c + 2]
            )[:, 0]

        @pl.when(has_up)
        def _():
            up_copy(up_s.at[slot], up_r.at[slot], slot).start()

        @pl.when(has_down)
        def _():
            down_copy(down_s.at[slot], down_r.at[slot], slot).start()

    def finish_faces(top, bottom, slot):
        count = top.shape[0]

        @pl.when(has_down)
        def _():
            up_copy(up_s.at[slot], up_r.at[slot], slot).wait_recv()

        @pl.when(has_up)
        def _():
            down_copy(down_s.at[slot], down_r.at[slot], slot).wait_recv()

        below = []
        above = []
        for pair in range(2):
            packed = up_r[slot, 0:count, pair : pair + 1]
            below += [roll_lane(packed, 64), packed]
            packed = down_r[slot, 0:count, pair : pair + 1]
            above += [packed, roll_lane(packed, 64)]
        below.append(from_right(below[0]))
        above.append(from_right(above[0]))
        below = jnp.concatenate(below, axis=1)
        above = jnp.concatenate(above, axis=1)
        new_top = top + pick(low_half, above, roll_lane(bottom, 64))
        new_bottom = bottom + pick(low_half, roll_lane(top, 64), below)
        return (new_top, new_bottom)

    materials = jnp.concatenate([lam_ref[...], mu_ref[...], rho_ref[...]], axis=1)
    moved = move_left(rows_ref[...], materials)
    cube = cube_ref[...]
    clam[...] = moved[:, 0:128].reshape(5, 5, 8, LANES) * cube
    cmu[...] = moved[:, 128:256].reshape(5, 5, 8, LANES) * cube
    mass = moved[:, 256:384].reshape(5, 5, 8, LANES) * cube
    mass = [assemble_xy(mass[a : a + 1]) for a in range(5)]
    mass_slot = steps * 2
    send_faces(mass[0], mass[4], mass_slot)

    elem = rec_elem_ref[...] - LANES * me
    lanes = lax.broadcasted_iota(jnp.int32, (32, LANES), 1)
    rec_lane = jnp.where(lanes == elem, 1.0, 0.0)
    off = rec_off_ref[0]
    row = off[:, 0:1] * 40 + off[:, 2:3] * 8 + off[:, 1:2]
    rec_rows = jnp.where(lax.broadcasted_iota(jnp.int32, (32, 200), 1) == row, 1.0, 0.0)
    rec_rows = rec_rows.astype(jnp.bfloat16)
    src_row = src_ref[1] * 40 + src_ref[3] * 8 + src_ref[2]
    src_lane = src_ref[0] - LANES * me

    @pl.when(has_down)
    def _():
        up_copy(halo_s, halo_r, halo_slot).wait_recv()

    for index, ref in enumerate(inputs):
        layer0 = ref[0, :, 0:5]
        layer1 = jnp.concatenate([ref[0, :, 4:8], halo_r[index][:, None]], axis=1)
        parts = []
        for layer in (layer0, layer1):
            for shifted in (layer, roll_sub(layer)):
                parts.append(shifted.reshape(120, LANES))
        moved = move_right(jnp.concatenate(parts, axis=1), spread_ref[...])
        for c in range(4):
            fields[index, :, :, c] = moved[:, c * LANES : (c + 1) * LANES].reshape(
                3, 5, 8, LANES
            )
        fields[index, :, :, 4] = from_right(
            moved[:, 0:LANES].reshape(3, 5, 8, LANES)
        )

    top, bottom = finish_faces(mass[0], mass[4], mass_slot)
    real_row = sub_iota(4) < 5
    for a in range(5):
        plane = top if a == 0 else (bottom if a == 4 else mass[a])
        keep = real_row
        if a == 4:
            keep = keep & ((lane_iota(4) < 64) | has_down)
        keep = jnp.broadcast_to(keep, plane.shape)
        safe = jnp.where(keep, plane, 1.0)
        minv[a] = jnp.where(keep, time_step**2 / safe, 0.0)[0]

    def strain_at(index, a):
        plane = fields[index, :, a]
        gx = []
        for c in range(5):
            total = None
            for k in range(5):
                if DERIV[c, k] == 0.0:
                    continue
                term = float(DERIV[c, k]) * plane[:, k]
                total = term if total is None else total + term
            gx.append(total[:, None])
        gx = jnp.concatenate(gx, axis=1)
        gy = None
        gz = None
        for k in range(5):
            row_k = jnp.broadcast_to(plane[:, :, k : k + 1], plane.shape)
            term = dy_ref[0, k] * row_k
            gy = term if gy is None else gy + term
            term = dz_ref[a * 5 + k] * fields[index, :, k]
            gz = term if gz is None else gz + term
        return (
            gx[0],
            gy[1],
            gz[2],
            gy[0] + gx[1],
            gz[0] + gx[2],
            gz[1] + gy[2],
        )

    def add_kernel(strain, a, moment):
        other = [strains[moment, a, i] for i in range(6)]
        div_a = strain[0] + strain[1] + strain[2]
        div_f = other[0] + other[1] + other[2]
        diag = strain[0] * other[0] + strain[1] * other[1] + strain[2] * other[2]
        shear = strain[3] * other[3] + strain[4] * other[4] + strain[5] * other[5]
        lam_part = div_a * div_f
        mu_part = diag + 0.5 * shear
        if moment == steps - 1:
            ksum[0, a] = lam_part
            ksum[1, a] = mu_part
        else:
            ksum[0, a] = ksum[0, a] + lam_part
            ksum[1, a] = ksum[1, a] + mu_part

    def run_step(index, slot, keep_strain, kernel_moment, load, beside):
        def stress_body(a, carry):
            strain = strain_at(index, a)
            lam_div = clam[a] * (strain[0] + strain[1] + strain[2])
            mu_a = cmu[a]
            mu_two = mu_a + mu_a
            for i in range(3):
                stress[i, a] = lam_div + mu_two * strain[i]
                stress[3 + i, a] = mu_a * strain[3 + i]
            if keep_strain is not None:
                for i in range(6):
                    strains[keep_strain, a, i] = strain[i]
            if kernel_moment is not None:
                add_kernel(strain, a, kernel_moment)
            return carry

        lax.fori_loop(0, 5, stress_body, 0)

        def force_body(a, carry):
            along = ((0, 3, 4), (3, 1, 5), (4, 5, 2))
            for comp in range(3):
                sx = stress[along[comp][0], a]
                sy = stress[along[comp][1], a]
                pieces = []
                for c in range(5):
                    total = None
                    for q in range(5):
                        if DERIV[q, c] == 0.0:
                            continue
                        term = float(DERIV[q, c]) * sx[q]
                        total = term if total is None else total + term
                    pieces.append(total[None])
                total = jnp.concatenate(pieces, axis=0)
                for q in range(5):
                    row_q = jnp.broadcast_to(sy[:, q : q + 1], sy.shape)
                    total = total + dy_ref[1, q] * row_q
                    total = total + dz_ref[25 + a * 5 + q] * stress[along[comp][2], q]
                force[comp, a] = total - load(comp, a)
            force[:, a] = assemble_xy(force[:, a])
            return carry

        lax.fori_loop(0, 5, force_body, 0)
        send_faces(force[:, 0], force[:, 4], slot)
        def inner(a, carry):
            fields[index + 1, :, a] = (
                2.0 * fields[index, :, a] - fields[index + 1, :, a]
            ) - minv[a] * force[:, a]
            return carry

        lax.fori_loop(1, 4, inner, 0)
        if beside is not None:
            beside()
        top, bottom = finish_faces(force[:, 0], force[:, 4], slot)
        for a, plane in ((0, top), (4, bottom)):
            fields[index + 1, :, a] = (
                2.0 * fields[index, :, a] - fields[index + 1, :, a]
            ) - minv[a] * plane

    def swap(index):
        def body(a, carry):
            held = fields[index, :, a]
            fields[index, :, a] = fields[index + 1, :, a]
            fields[index + 1, :, a] = held
            return carry

        lax.fori_loop(0, 5, body, 0)

    def record(moment):
        values = jnp.concatenate(
            [fields[0, comp].reshape(200, LANES) for comp in range(3)], axis=1
        )
        at_rows = move_left(rec_rows, values)
        found = []
        for comp in range(3):
            seen = at_rows[:, comp * LANES : (comp + 1) * LANES] * rec_lane
            found.append(
                jnp.sum(seen, axis=1, keepdims=True)
                - data_ref[0, moment, :, comp : comp + 1]
            )
        return found

    residuals = []

    for moment in range(steps):
        def source_load(comp, a, moment=moment):
            here = (lax.broadcasted_iota(jnp.int32, (5, 8, LANES), 0) * 8
                    + lax.broadcasted_iota(jnp.int32, (5, 8, LANES), 1)
                    + a * 40) == src_row
            there = lax.broadcasted_iota(jnp.int32, (5, 8, LANES), 2) == src_lane
            return jnp.where(here & there, force_ref[moment * 3 + comp], 0.0)

        def beside(moment=moment):
            if moment > 0:
                residuals.append(record(moment - 1))

        run_step(
            0, moment, moment - 1 if moment > 0 else None, None, source_load, beside
        )
        swap(0)
    residuals.append(record(steps - 1))

    def last_strain(a, carry):
        strain = strain_at(0, a)
        for i in range(6):
            strains[steps - 1, a, i] = strain[i]
        return carry

    lax.fori_loop(0, 5, last_strain, 0)

    def put_out(index, ref):
        sides = [fields[index, :, 0:4, c].reshape(96, LANES) for c in range(4)]
        moved = move_right(jnp.concatenate(sides, axis=1), gather_ref[...])
        for ez in range(2):
            first = moved[:, 2 * ez * LANES : (2 * ez + 1) * LANES]
            second = moved[:, (2 * ez + 1) * LANES : (2 * ez + 2) * LANES]
            first = first.reshape(3, 4, 8, LANES)
            second = roll_sub(second.reshape(3, 4, 8, LANES))
            ref[0, :, 4 * ez : 4 * ez + 4] = pick(sub_iota(4) < 4, first, second)

    for moment in reversed(range(steps)):
        scaled = jnp.concatenate(
            [adjoint_gain * residuals[moment][comp] * rec_lane for comp in range(3)],
            axis=1,
        )
        high, middle, low = split3(scaled)
        contract = (((0,), (0,)), ((), ()))
        spreaded = sum(
            lax.dot_general(
                rec_rows, part, contract, preferred_element_type=jnp.float32
            )
            for part in (high, middle, low)
        )
        for comp in range(3):
            clamped = spreaded[:, comp * LANES : (comp + 1) * LANES]
            ev_load = clamped.reshape(5, 5, 8, LANES)
            force[comp] = ev_load

        def beside(moment=moment):
            if moment == steps - 1:
                put_out(0, final_f_ref)

        run_step(
            2,
            2 * steps - 1 - moment,
            None,
            moment,
            lambda comp, a: force[comp, a],
            beside,
        )
        swap(2)

    both = jnp.concatenate(
        [ksum[0].reshape(200, LANES), ksum[1].reshape(200, LANES)], axis=1
    )
    natural = move_left(rows_t_ref[...], both)
    width = LANES // n_event
    k_lam = natural[:, 0:LANES] * (-time_step * lam_ref[...])
    k_mu = natural[:, LANES : 2 * LANES] * (-2.0 * time_step * mu_ref[...])
    lane2 = lax.broadcasted_iota(jnp.int32, (125, LANES), 1)

    def packed_for(target):
        shift = lax.rem(LANES - width * target, LANES)
        return jnp.where(
            lane2 < width,
            pltpu.roll(k_lam, shift, 1),
            pltpu.roll(k_mu, lax.rem(shift + width, LANES), 1),
        )

    def event_copy(hop):
        return pltpu.make_async_remote_copy(
            src_ref=ev_s.at[hop - 1], dst_ref=ev_r.at[hop - 1],
            send_sem=s_ev.at[hop - 1], recv_sem=r_ev.at[hop - 1],
            device_id={"event": lax.rem(event + hop, n_event)},
        )

    for hop in range(1, n_event):
        ev_s[hop - 1] = packed_for(lax.rem(event + hop, n_event))
        event_copy(hop).start()
    put_out(2, final_a_ref)
    total = packed_for(event)
    for hop in range(1, n_event):
        event_copy(hop).wait_recv()
        total = total + ev_r[hop - 1]
    out_ref[0] = total[:, 0:width]
    out_ref[1] = total[:, width : 2 * width]

    @pl.when(has_up)
    def _():
        up_copy(halo_s, halo_r, halo_slot).wait_send()
        for slot in range(2 * steps + 1):
            up_copy(up_s.at[slot], up_r.at[slot], slot).wait_send()

    @pl.when(has_down)
    def _():
        for slot in range(2 * steps + 1):
            down_copy(down_s.at[slot], down_r.at[slot], slot).wait_send()

    for hop in range(1, n_event):
        event_copy(hop).wait_send()


def on_device(
    n_mesh,
    n_event,
    forward_before,
    forward_now,
    adjoint_after,
    adjoint_now,
    mass_density,
    lame_lambda,
    lame_mu,
    source_element,
    source_offset,
    source_force,
    receiver_element,
    receiver_offset,
    receiver_data,
):
    assert forward_now.shape[1:] == (3, 8, 8, 128)
    assert lame_mu.shape == (125, 128)
    steps = source_force.shape[1]
    source = jnp.concatenate([source_element, source_offset[0]])
    field = forward_now.shape
    vmem = pl.BlockSpec(memory_space=pltpu.VMEM)
    smem = pl.BlockSpec(memory_space=pltpu.SMEM)
    f32 = jnp.float32
    elem = (5, 5, 8, LANES)
    slots = 2 * steps + 1
    return pl.pallas_call(
        functools.partial(kernel, n_mesh, n_event, steps),
        out_shape=(
            jax.ShapeDtypeStruct(field, f32),
            jax.ShapeDtypeStruct(field, f32),
            jax.ShapeDtypeStruct((2, 125, LANES // n_event), f32),
        ),
        in_specs=[vmem] * 7 + [smem, smem] + [vmem] * 3 + [vmem] * 6 + [smem],
        out_specs=(vmem, vmem, vmem),
        scratch_shapes=[
            pltpu.VMEM((4, 3) + elem, f32),
            pltpu.VMEM((6,) + elem, f32),
            pltpu.VMEM((3,) + elem, f32),
            pltpu.VMEM((steps, 5, 6, 5, 8, LANES), f32),
            pltpu.VMEM((2,) + elem, f32),
            pltpu.VMEM(elem, f32),
            pltpu.VMEM(elem, f32),
            pltpu.VMEM(elem, f32),
            pltpu.VMEM((4, 3, 8, LANES), f32),
            pltpu.VMEM((4, 3, 8, LANES), f32),
            pltpu.VMEM((slots, 3, 2, 8, LANES), f32),
            pltpu.VMEM((slots, 3, 2, 8, LANES), f32),
            pltpu.VMEM((slots, 3, 2, 8, LANES), f32),
            pltpu.VMEM((slots, 3, 2, 8, LANES), f32),
            pltpu.VMEM((max(1, n_event - 1), 125, LANES), f32),
            pltpu.VMEM((max(1, n_event - 1), 125, LANES), f32),
            pltpu.SemaphoreType.DMA((slots + 1,)),
            pltpu.SemaphoreType.DMA((slots + 1,)),
            pltpu.SemaphoreType.DMA((slots,)),
            pltpu.SemaphoreType.DMA((slots,)),
            pltpu.SemaphoreType.DMA((max(1, n_event - 1),)),
            pltpu.SemaphoreType.DMA((max(1, n_event - 1),)),
        ],
        compiler_params=pltpu.CompilerParams(
            collective_id=0, has_side_effects=True, vmem_limit_bytes=48 * 1024 * 1024
        ),
    )(
        forward_now,
        forward_before,
        adjoint_now,
        adjoint_after,
        mass_density,
        lame_lambda,
        lame_mu,
        source,
        source_force.reshape(-1),
        receiver_element.reshape(-1, 1),
        receiver_offset,
        receiver_data,
        *constants(),
    )


def solution(mesh):
    return jax.shard_map(
        functools.partial(on_device, mesh.shape["mesh"], mesh.shape["event"]),
        mesh=mesh,
        in_specs=(
            P("event", None, "mesh", None, None),
            P("event", None, "mesh", None, None),
            P("event", None, "mesh", None, None),
            P("event", None, "mesh", None, None),
            P(None, "mesh"),
            P(None, "mesh"),
            P(None, "mesh"),
            P("event"),
            P("event", None),
            P("event", None, None),
            P("event", None),
            P("event", None, None),
            P("event", None, None, None),
        ),
        out_specs=(
            P("event", None, "mesh", None, None),
            P("event", None, "mesh", None, None),
            P(None, None, ("mesh", "event")),
        ),
        check_vma=False,
    )
```

profile of v0, /device:TPU:24, one launch (start us, length us, event | category | flops | bytes accessed | tf_op | source)
XLA Modules:
  0.0 57.9 jit_solution(16061130666150041797)
XLA Ops:
  0.6 0.0 copy-start.2
  1.3 0.7 %pad_add_fusion.src_ref = s32[4]{0:T(128)S(1)} fusion(s32[3]{0:T(128)} %bitcast.3, s32[1]{0:T(128)S(6)} %copy.29), kind=kLoop, calls=%fused_computation | loop fusion | flops 4 | bytes 32 | tf_op jit(solution)/shard_map/concatenate | solution.py:599
  2.1 0.7 %reduce = f32[3,3]{1,0:T(4,128)S(1)} reduce(f32[1,3,3]{2,0,1:T(1,128)} %param.29, f32[]{:T(128)} %constant.31), dimensions={0}, to_apply=%param.29.reduce_sub_computation | reduce | bytes 76 | tf_op args[9]
  2.8 0.1 reshape.12.force_ref
  2.8 0.7 %copy.23.rec_elem_ref = s32[32,1]{1,0:T(8,128)S(1)} copy(s32[32,1]{0,1:T(1,128)} %bitcast.2) | data formatting | bytes 256 | tf_op jit(solution)/shard_map/reshape | solution.py:652
  3.6 0.8 %copy.24.rec_off_ref = s32[1,32,3]{2,1,0:T(8,128)S(1)} copy(s32[1,32,3]{1,0,2:T(1,128)} %param.31) | data formatting | bytes 768 | tf_op args[11]
  4.3 0.0 copy-start.13
  4.3 0.8 %copy.25.data_ref = f32[1,3,32,3]{3,2,1,0:T(8,128)S(1)} copy(f32[1,3,32,3]{2,0,3,1:T(1,128)} %param.32) | data formatting | bytes 2304 | tf_op args[12]
  5.1 0.0 copy-done.2
  5.1 0.0 copy-done.13
  5.1 0.0 copy-start
  5.2 1.0 %copy-done = bf16[512,512]{1,0:T(8,128)(2,1)S(1)} copy-done((bf16[512,512]{1,0:T(8,128)(2,1)S(1)}, bf16[512,512]{1,0:T(8,128)(2,1)}, u32[]{:S(2)}) %copy-start) | copy-done | bytes 524312
  6.2 1.0 %copy-done.1 = bf16[512,512]{1,0:T(8,128)(2,1)S(1)} copy-done((bf16[512,512]{1,0:T(8,128)(2,1)S(1)}, bf16[512,512]{1,0:T(8,128)(2,1)}, u32[]{:S(2)}) %copy-start.1) | copy-done | bytes 524312
  7.2 0.0 copy-start.3
  7.2 0.9 %copy-done.3 = f32[1,3,8,8,128]{4,3,2,1,0:T(8,128)S(1)} copy-done((f32[1,3,8,8,128]{4,3,2,1,0:T(8,128)S(1)}, f32[1,3,8,8,128]{4,3,2,1,0:T(8,128)}, u32[]{:S(2)}) %copy-start.3) | copy-done | bytes 98328
  8.1 0.0 copy-start.4
  8.1 0.9 %copy-done.4 = f32[1,3,8,8,128]{4,3,2,1,0:T(8,128)S(1)} copy-done((f32[1,3,8,8,128]{4,3,2,1,0:T(8,128)S(1)}, f32[1,3,8,8,128]{4,3,2,1,0:T(8,128)}, u32[]{:S(2)}) %copy-start.4) | copy-done | bytes 98328
  9.0 0.0 copy-start.5
  9.0 0.9 %copy-done.5 = f32[1,3,8,8,128]{4,3,2,1,0:T(8,128)S(1)} copy-done((f32[1,3,8,8,128]{4,3,2,1,0:T(8,128)S(1)}, f32[1,3,8,8,128]{4,3,2,1,0:T(8,128)}, u32[]{:S(2)}) %copy-start.5) | copy-done | bytes 98328
  9.9 0.0 copy-start.6
  9.9 0.9 %copy-done.6 = f32[1,3,8,8,128]{4,3,2,1,0:T(8,128)S(1)} copy-done((f32[1,3,8,8,128]{4,3,2,1,0:T(8,128)S(1)}, f32[1,3,8,8,128]{4,3,2,1,0:T(8,128)}, u32[]{:S(2)}) %copy-start.6) | copy-done | bytes 98328
  10.8 0.0 copy-start.7
  10.8 0.8 %copy-done.7 = f32[125,128]{1,0:T(8,128)S(1)} copy-done((f32[125,128]{1,0:T(8,128)S(1)}, f32[125,128]{1,0:T(8,128)}, u32[]{:S(2)}) %copy-start.7) | copy-done | bytes 64024
  11.6 0.8 %copy-done.8 = f32[125,128]{1,0:T(8,128)S(1)} copy-done((f32[125,128]{1,0:T(8,128)S(1)}, f32[125,128]{1,0:T(8,128)}, u32[]{:S(2)}) %copy-start.8) | copy-done | bytes 64024
  12.5 0.8 %copy-done.9 = f32[125,128]{1,0:T(8,128)S(1)} copy-done((f32[125,128]{1,0:T(8,128)S(1)}, f32[125,128]{1,0:T(8,128)}, u32[]{:S(2)}) %copy-start.9) | copy-done | bytes 64024
  13.3 0.8 %copy-done.10 = bf16[125,200]{1,0:T(8,128)(2,1)S(1)} copy-done((bf16[125,200]{1,0:T(8,128)(2,1)S(1)}, bf16[125,200]{1,0:T(8,128)(2,1)}, u32[]{:S(2)}) %copy-start.10) | copy-done | bytes 50024
  14.2 0.8 %copy-done.11 = bf16[200,125]{1,0:T(8,128)(2,1)S(1)} copy-done((bf16[200,125]{1,0:T(8,128)(2,1)S(1)}, bf16[200,125]{1,0:T(8,128)(2,1)}, u32[]{:S(2)}) %copy-start.11) | copy-done | bytes 50024
  15.0 0.8 %copy-done.12 = f32[2,5,8,128]{3,2,1,0:T(8,128)S(1)} copy-done((f32[2,5,8,128]{3,2,1,0:T(8,128)S(1)}, f32[2,5,8,128]{3,2,1,0:T(8,128)}, u32[]{:S(2)}) %copy-start.12) | copy-done | bytes 40984
  15.7 40.2 %shard_map.211 = (f32[1,3,8,8,128]{4,3,2,1,0:T(8,128)S(1)}, f32[1,3,8,8,128]{4,3,2,1,0:T(8,128)S(1)}, f32[2,125,64]{2,1,0:T(8,128)S(1)}) custom-call(f32[1,3,8,8,128]{4,3,2,1,0:T(8,128)S(1)} %copy-done.3, f32[1,3,8,8,128]{4,3,2,1,0:T(8,128)S(1)} %copy-done.4, f32[1,3,8,8,128]{4,3,2,1,0:T(8,128)S(1)} %copy-done.5, f32[1,3,8,8,128]{4,3,2,1,0:T(8,128)S(1)} %copy-done.6, ...), custom_call_target="tpu_custom_call" | custom-call | tf_op jit(solution)/shard_map/pallas_call | solution.py:606
  55.9 0.7 %copy.26 = f32[2,125,64]{1,2,0:T(8,128)} copy(f32[2,125,64]{2,1,0:T(8,128)S(1)} %get-tuple-element.5) | data formatting | bytes 128000 | tf_op jit(solution)/shard_map/pallas_call | solution.py:606
  56.7 0.6 %copy.30 = f32[1,3,8,8,128]{4,3,2,1,0:T(8,128)} copy(f32[1,3,8,8,128]{4,3,2,1,0:T(8,128)S(1)} %get-tuple-element.9) | data formatting | bytes 196608
  57.3 0.6 %copy.31 = f32[1,3,8,8,128]{4,3,2,1,0:T(8,128)} copy(f32[1,3,8,8,128]{4,3,2,1,0:T(8,128)S(1)} %get-tuple-element.10) | data formatting | bytes 196608
  (6 shorter events, 0.0 us)
Async XLA Ops:
  0.6 4.5 %copy-start.2 = (f32[5,5,8,128]{3,2,1,0:T(8,128)S(1)}, f32[5,5,8,128]{3,2,1,0:T(8,128)}, u32[]{:S(2)}) copy-start(f32[5,5,8,128]{3,2,1,0:T(8,128)} %constant.18.clone.cube_ref) | copy-start | bytes 307204
  4.3 0.8 %copy-start.13 = (f32[50]{0:T(128)S(1)}, f32[50]{0:T(128)}, u32[]{:S(2)}) copy-start(f32[50]{0:T(128)} %constant.20.clone.dz_ref) | copy-start | bytes 604
  5.1 1.0 %copy-start = (bf16[512,512]{1,0:T(8,128)(2,1)S(1)}, bf16[512,512]{1,0:T(8,128)(2,1)}, u32[]{:S(2)}) copy-start(bf16[512,512]{1,0:T(8,128)(2,1)} %constant.15.clone.gather_ref) | copy-start | bytes 1572868
  6.2 1.0 %copy-start.1 = (bf16[512,512]{1,0:T(8,128)(2,1)S(1)}, bf16[512,512]{1,0:T(8,128)(2,1)}, u32[]{:S(2)}) copy-start(bf16[512,512]{1,0:T(8,128)(2,1)} %constant.14.clone.spread_ref) | copy-start | bytes 1572868
  7.2 0.9 %copy-start.3 = (f32[1,3,8,8,128]{4,3,2,1,0:T(8,128)S(1)}, f32[1,3,8,8,128]{4,3,2,1,0:T(8,128)}, u32[]{:S(2)}) copy-start(f32[1,3,8,8,128]{4,3,2,1,0:T(8,128)} %now_ref.1) | copy-start | bytes 294916
  8.1 0.9 %copy-start.4 = (f32[1,3,8,8,128]{4,3,2,1,0:T(8,128)S(1)}, f32[1,3,8,8,128]{4,3,2,1,0:T(8,128)}, u32[]{:S(2)}) copy-start(f32[1,3,8,8,128]{4,3,2,1,0:T(8,128)} %before_ref.1) | copy-start | bytes 294916
  9.0 0.9 %copy-start.5 = (f32[1,3,8,8,128]{4,3,2,1,0:T(8,128)S(1)}, f32[1,3,8,8,128]{4,3,2,1,0:T(8,128)}, u32[]{:S(2)}) copy-start(f32[1,3,8,8,128]{4,3,2,1,0:T(8,128)} %adj_ref.1) | copy-start | bytes 294916
  9.9 0.9 %copy-start.6 = (f32[1,3,8,8,128]{4,3,2,1,0:T(8,128)S(1)}, f32[1,3,8,8,128]{4,3,2,1,0:T(8,128)}, u32[]{:S(2)}) copy-start(f32[1,3,8,8,128]{4,3,2,1,0:T(8,128)} %after_ref.1) | copy-start | bytes 294916
  10.8 0.8 %copy-start.7 = (f32[125,128]{1,0:T(8,128)S(1)}, f32[125,128]{1,0:T(8,128)}, u32[]{:S(2)}) copy-start(f32[125,128]{1,0:T(8,128)} %rho_ref.1) | copy-start | bytes 192004
  11.6 0.8 %copy-start.8 = (f32[125,128]{1,0:T(8,128)S(1)}, f32[125,128]{1,0:T(8,128)}, u32[]{:S(2)}) copy-start(f32[125,128]{1,0:T(8,128)} %lam_ref.1) | copy-start | bytes 192004
  12.5 0.8 %copy-start.9 = (f32[125,128]{1,0:T(8,128)S(1)}, f32[125,128]{1,0:T(8,128)}, u32[]{:S(2)}) copy-start(f32[125,128]{1,0:T(8,128)} %mu_ref.1) | copy-start | bytes 192004
  13.3 0.8 %copy-start.10 = (bf16[125,200]{1,0:T(8,128)(2,1)S(1)}, bf16[125,200]{1,0:T(8,128)(2,1)}, u32[]{:S(2)}) copy-start(bf16[125,200]{1,0:T(8,128)(2,1)} %constant.17.clone.rows_t_ref) | copy-start | bytes 150004
  14.2 0.8 %copy-start.11 = (bf16[200,125]{1,0:T(8,128)(2,1)S(1)}, bf16[200,125]{1,0:T(8,128)(2,1)}, u32[]{:S(2)}) copy-start(bf16[200,125]{1,0:T(8,128)(2,1)} %constant.16.clone.rows_ref) | copy-start | bytes 150004
  15.0 0.8 %copy-start.12 = (f32[2,5,8,128]{3,2,1,0:T(8,128)S(1)}, f32[2,5,8,128]{3,2,1,0:T(8,128)}, u32[]{:S(2)}) copy-start(f32[2,5,8,128]{3,2,1,0:T(8,128)} %constant.19.clone.dy_ref) | copy-start | bytes 122884
where the time goes:
time: 58.7 us; the launch traced here: 57.9 us
  Pallas kernels  40.2 us (68%)
  local copies, waits for them, and re-layouts  15 us (26%)
  other arithmetic  1.43 us (2%)
  between operations  1.35 us (2%)
    pallas_call x1, Pallas kernels, on_device(): pl.pallas_call(functools.partial(kernel, n_mesh, n_event, steps), out_sha...  40.2 us
    unnamed x32, local copies, waits for them, and re-layouts  13.4 us

commit v1 on v0

--- a/solution.py
+++ b/solution.py
@@ -59,7 +59,6 @@
         jnp.asarray(spread, bf),
         jnp.asarray(np.ascontiguousarray(spread.T), bf),
         jnp.asarray(rows, bf),
-        jnp.asarray(np.ascontiguousarray(rows.T), bf),
         jnp.asarray(cube),
         jnp.asarray(dy),
         jnp.asarray(dz),
@@ -79,13 +78,24 @@
 
 
 def move_right(values, table):
-    high, middle, low = split3(values)
-    return dot(high, table) + dot(middle, table) + dot(low, table)
+    parts = split3(values)
+    count = values.shape[0]
+    stacked = jnp.concatenate(parts, axis=0)
+    moved = dot(stacked, table)
+    return moved[0:count] + moved[count : 2 * count] + moved[2 * count : 3 * count]
 
 
 def move_left(table, values):
     high, middle, low = split3(values)
     return dot(table, high) + dot(table, middle) + dot(table, low)
+
+
+def move_left_t(table, values):
+    contract = (((0,), (0,)), ((), ()))
+    return sum(
+        lax.dot_general(table, part, contract, preferred_element_type=jnp.float32)
+        for part in split3(values)
+    )
 
 
 def roll_lane(value, shift):
@@ -132,6 +142,28 @@
     n_mesh,
     n_event,
     steps,
+    now_hbm,
+    before_hbm,
+    adj_hbm,
+    after_hbm,
+    rho_hbm,
+    lam_hbm,
+    mu_hbm,
+    rec_elem_hbm,
+    rec_off_hbm,
+    data_hbm,
+    spread_hbm,
+    gather_hbm,
+    rows_hbm,
+    cube_hbm,
+    dy_hbm,
+    elem_ref,
+    off_ref,
+    force_ref,
+    dz_ref,
+    final_f_ref,
+    final_a_ref,
+    out_ref,
     now_ref,
     before_ref,
     adj_ref,
@@ -139,25 +171,20 @@
     rho_ref,
     lam_ref,
     mu_ref,
-    src_ref,
-    force_ref,
     rec_elem_ref,
     rec_off_ref,
     data_ref,
     spread_ref,
     gather_ref,
     rows_ref,
-    rows_t_ref,
     cube_ref,
     dy_ref,
-    dz_ref,
-    final_f_ref,
-    final_a_ref,
-    out_ref,
+    s_in,
     fields,
     stress,
     force,
     strains,
+    astrain,
     ksum,
     clam,
     cmu,
@@ -182,6 +209,29 @@
     has_up = me > 0
     has_down = me < n_mesh - 1
 
+    loads = []
+    pairs = (
+        (now_hbm, now_ref),
+        (before_hbm, before_ref),
+        (adj_hbm, adj_ref),
+        (after_hbm, after_ref),
+        (rows_hbm, rows_ref),
+        (lam_hbm, lam_ref),
+        (mu_hbm, mu_ref),
+        (rho_hbm, rho_ref),
+        (cube_hbm, cube_ref),
+        (spread_hbm, spread_ref),
+        (dy_hbm, dy_ref),
+        (rec_elem_hbm, rec_elem_ref),
+        (rec_off_hbm, rec_off_ref),
+        (data_hbm, data_ref),
+        (gather_hbm, gather_ref),
+    )
+    for place, (source, target) in enumerate(pairs):
+        load_copy = pltpu.make_async_copy(source, target, s_in.at[place])
+        load_copy.start()
+        loads.append(load_copy)
+
     barrier = pltpu.get_barrier_semaphore()
 
     @pl.when(has_up)
@@ -198,6 +248,8 @@
         )
 
     inputs = (now_ref, before_ref, adj_ref, after_ref)
+    for place in range(4):
+        loads[place].wait()
     for index, ref in enumerate(inputs):
         halo_s[index] = ref[0, :, 0]
 
@@ -280,6 +332,8 @@
         new_bottom = bottom + pick(low_half, roll_lane(top, 64), below)
         return (new_top, new_bottom)
 
+    for place in range(4, 9):
+        loads[place].wait()
     materials = jnp.concatenate([lam_ref[...], mu_ref[...], rho_ref[...]], axis=1)
     moved = move_left(rows_ref[...], materials)
     cube = cube_ref[...]
@@ -290,21 +344,41 @@
     mass_slot = steps * 2
     send_faces(mass[0], mass[4], mass_slot)
 
+    for place in range(9, 14):
+        loads[place].wait()
+    nrec = rec_elem_ref.shape[1]
     elem = rec_elem_ref[...] - LANES * me
-    lanes = lax.broadcasted_iota(jnp.int32, (32, LANES), 1)
-    rec_lane = jnp.where(lanes == elem, 1.0, 0.0)
-    off = rec_off_ref[0]
-    row = off[:, 0:1] * 40 + off[:, 2:3] * 8 + off[:, 1:2]
-    rec_rows = jnp.where(lax.broadcasted_iota(jnp.int32, (32, 200), 1) == row, 1.0, 0.0)
-    rec_rows = rec_rows.astype(jnp.bfloat16)
-    src_row = src_ref[1] * 40 + src_ref[3] * 8 + src_ref[2]
-    src_lane = src_ref[0] - LANES * me
+    lane_t = lax.broadcasted_iota(jnp.int32, (LANES, nrec), 0) == elem
+    lane_t = jnp.where(lane_t, 1.0, 0.0).astype(jnp.bfloat16)
+    eye = jnp.where(
+        lax.broadcasted_iota(jnp.int32, (nrec, nrec), 0)
+        == lax.broadcasted_iota(jnp.int32, (nrec, nrec), 1),
+        1.0,
+        0.0,
+    ).astype(jnp.bfloat16)
+    turned = (((1,), (1,)), ((), ()))
+
+    def turn(part):
+        return lax.dot_general(eye, part, turned, preferred_element_type=jnp.float32)
+
+    rec_lane = turn(lane_t)
+    row = rec_off_ref[0] * 40 + rec_off_ref[2] * 8 + rec_off_ref[1]
+    rows_lanes = lax.broadcasted_iota(jnp.int32, (200, nrec), 0) == row
+    rows_lanes = jnp.where(rows_lanes, 1.0, 0.0).astype(jnp.bfloat16)
+    rec_rows = turn(rows_lanes).astype(jnp.bfloat16)
+    observed = jnp.concatenate(
+        [data_ref[n, comp] for n in range(steps) for comp in range(3)], axis=0
+    )
+    observed = sum(turn(part) for part in split3(observed))
+    src_row = off_ref[0, 0] * 40 + off_ref[0, 2] * 8 + off_ref[0, 1]
+    src_lane = elem_ref[0] - LANES * me
 
     @pl.when(has_down)
     def _():
         up_copy(halo_s, halo_r, halo_slot).wait_recv()
 
-    for index, ref in enumerate(inputs):
+    def bring_in(index):
+        ref = inputs[index]
         layer0 = ref[0, :, 0:5]
         layer1 = jnp.concatenate([ref[0, :, 4:8], halo_r[index][:, None]], axis=1)
         parts = []
@@ -320,16 +394,19 @@
             moved[:, 0:LANES].reshape(3, 5, 8, LANES)
         )
 
-    top, bottom = finish_faces(mass[0], mass[4], mass_slot)
-    real_row = sub_iota(4) < 5
-    for a in range(5):
-        plane = top if a == 0 else (bottom if a == 4 else mass[a])
-        keep = real_row
-        if a == 4:
-            keep = keep & ((lane_iota(4) < 64) | has_down)
-        keep = jnp.broadcast_to(keep, plane.shape)
-        safe = jnp.where(keep, plane, 1.0)
-        minv[a] = jnp.where(keep, time_step**2 / safe, 0.0)[0]
+    def finish_mass():
+        top, bottom = finish_faces(mass[0], mass[4], mass_slot)
+        real_row = sub_iota(4) < 5
+        for a in range(5):
+            plane = top if a == 0 else (bottom if a == 4 else mass[a])
+            keep = real_row
+            if a == 4:
+                keep = keep & ((lane_iota(4) < 64) | has_down)
+            keep = jnp.broadcast_to(keep, plane.shape)
+            safe = jnp.where(keep, plane, 1.0)
+            minv[a] = jnp.where(keep, time_step**2 / safe, 0.0)[0]
+
+    bring_in(0)
 
     def strain_at(index, a):
         plane = fields[index, :, a]
@@ -360,22 +437,30 @@
             gz[1] + gy[2],
         )
 
-    def add_kernel(strain, a, moment):
-        other = [strains[moment, a, i] for i in range(6)]
-        div_a = strain[0] + strain[1] + strain[2]
-        div_f = other[0] + other[1] + other[2]
-        diag = strain[0] * other[0] + strain[1] * other[1] + strain[2] * other[2]
-        shear = strain[3] * other[3] + strain[4] * other[4] + strain[5] * other[5]
-        lam_part = div_a * div_f
-        mu_part = diag + 0.5 * shear
-        if moment == steps - 1:
-            ksum[0, a] = lam_part
-            ksum[1, a] = mu_part
-        else:
-            ksum[0, a] = ksum[0, a] + lam_part
-            ksum[1, a] = ksum[1, a] + mu_part
-
-    def run_step(index, slot, keep_strain, kernel_moment, load, beside):
+    def add_kernels(moment, last_index):
+        def body(a, carry):
+            strain = [astrain[a, i] for i in range(6)]
+            if last_index is None:
+                other = [strains[moment, a, i] for i in range(6)]
+            else:
+                other = strain_at(last_index, a)
+            div_a = strain[0] + strain[1] + strain[2]
+            div_f = other[0] + other[1] + other[2]
+            diag = strain[0] * other[0] + strain[1] * other[1] + strain[2] * other[2]
+            shear = strain[3] * other[3] + strain[4] * other[4] + strain[5] * other[5]
+            lam_part = div_a * div_f
+            mu_part = diag + 0.5 * shear
+            if last_index is not None:
+                ksum[0, a] = lam_part
+                ksum[1, a] = mu_part
+            else:
+                ksum[0, a] = ksum[0, a] + lam_part
+                ksum[1, a] = ksum[1, a] + mu_part
+            return carry
+
+        lax.fori_loop(0, 5, body, 0)
+
+    def run_step(index, older, slot, keep_strain, load, beside):
         def stress_body(a, carry):
             strain = strain_at(index, a)
             lam_div = clam[a] * (strain[0] + strain[1] + strain[2])
@@ -386,9 +471,7 @@
                 stress[3 + i, a] = mu_a * strain[3 + i]
             if keep_strain is not None:
                 for i in range(6):
-                    strains[keep_strain, a, i] = strain[i]
-            if kernel_moment is not None:
-                add_kernel(strain, a, kernel_moment)
+                    keep_strain[a, i] = strain[i]
             return carry
 
         lax.fori_loop(0, 5, stress_body, 0)
@@ -418,33 +501,24 @@
 
         lax.fori_loop(0, 5, force_body, 0)
         send_faces(force[:, 0], force[:, 4], slot)
+        beside()
+
         def inner(a, carry):
-            fields[index + 1, :, a] = (
-                2.0 * fields[index, :, a] - fields[index + 1, :, a]
+            fields[older, :, a] = (
+                2.0 * fields[index, :, a] - fields[older, :, a]
             ) - minv[a] * force[:, a]
             return carry
 
         lax.fori_loop(1, 4, inner, 0)
-        if beside is not None:
-            beside()
         top, bottom = finish_faces(force[:, 0], force[:, 4], slot)
         for a, plane in ((0, top), (4, bottom)):
-            fields[index + 1, :, a] = (
-                2.0 * fields[index, :, a] - fields[index + 1, :, a]
+            fields[older, :, a] = (
+                2.0 * fields[index, :, a] - fields[older, :, a]
             ) - minv[a] * plane
 
-    def swap(index):
-        def body(a, carry):
-            held = fields[index, :, a]
-            fields[index, :, a] = fields[index + 1, :, a]
-            fields[index + 1, :, a] = held
-            return carry
-
-        lax.fori_loop(0, 5, body, 0)
-
-    def record(moment):
+    def record(index, moment):
         values = jnp.concatenate(
-            [fields[0, comp].reshape(200, LANES) for comp in range(3)], axis=1
+            [fields[index, comp].reshape(200, LANES) for comp in range(3)], axis=1
         )
         at_rows = move_left(rec_rows, values)
         found = []
@@ -452,37 +526,44 @@
             seen = at_rows[:, comp * LANES : (comp + 1) * LANES] * rec_lane
             found.append(
                 jnp.sum(seen, axis=1, keepdims=True)
-                - data_ref[0, moment, :, comp : comp + 1]
+                - observed[:, 3 * moment + comp : 3 * moment + comp + 1]
             )
         return found
 
     residuals = []
 
+    index, older = 0, 1
     for moment in range(steps):
         def source_load(comp, a, moment=moment):
             here = (lax.broadcasted_iota(jnp.int32, (5, 8, LANES), 0) * 8
                     + lax.broadcasted_iota(jnp.int32, (5, 8, LANES), 1)
                     + a * 40) == src_row
             there = lax.broadcasted_iota(jnp.int32, (5, 8, LANES), 2) == src_lane
-            return jnp.where(here & there, force_ref[moment * 3 + comp], 0.0)
-
-        def beside(moment=moment):
-            if moment > 0:
-                residuals.append(record(moment - 1))
+            return jnp.where(here & there, force_ref[moment, 0, comp], 0.0)
+
+        def beside(moment=moment, index=index):
+            if moment == 0:
+                bring_in(1)
+                finish_mass()
+            else:
+                residuals.append(record(index, moment - 1))
+            if moment == min(1, steps - 1):
+                bring_in(2)
+            if moment == steps - 1:
+                bring_in(3)
 
         run_step(
-            0, moment, moment - 1 if moment > 0 else None, None, source_load, beside
-        )
-        swap(0)
-    residuals.append(record(steps - 1))
-
-    def last_strain(a, carry):
-        strain = strain_at(0, a)
-        for i in range(6):
-            strains[steps - 1, a, i] = strain[i]
-        return carry
-
-    lax.fori_loop(0, 5, last_strain, 0)
+            index,
+            older,
+            moment,
+            strains.at[moment - 1] if moment > 0 else None,
+            source_load,
+            beside,
+        )
+        index, older = older, index
+    residuals.append(record(index, steps - 1))
+    last_forward = index
+    loads[14].wait()
 
     def put_out(index, ref):
         sides = [fields[index, :, 0:4, c].reshape(96, LANES) for c in range(4)]
@@ -494,72 +575,62 @@
             second = roll_sub(second.reshape(3, 4, 8, LANES))
             ref[0, :, 4 * ez : 4 * ez + 4] = pick(sub_iota(4) < 4, first, second)
 
+    width = LANES // n_event
+
+    def event_copy(hop):
+        target = lax.rem(event + hop, n_event)
+        return pltpu.make_async_remote_copy(
+            src_ref=ev_s.at[:, pl.ds(pl.multiple_of(width * target, width), width)],
+            dst_ref=ev_r.at[hop - 1],
+            send_sem=s_ev.at[hop - 1],
+            recv_sem=r_ev.at[hop - 1],
+            device_id={"event": target},
+        )
+
+    def send_kernels():
+        scales = (-time_step, -2.0 * time_step)
+        for which, modulus in enumerate((lam_ref, mu_ref)):
+            natural = move_left_t(rows_ref[...], ksum[which].reshape(200, LANES))
+            ev_s[which] = jnp.transpose(natural * (scales[which] * modulus[...]))
+        for hop in range(1, n_event):
+            event_copy(hop).start()
+
+    index, older = 2, 3
     for moment in reversed(range(steps)):
         scaled = jnp.concatenate(
             [adjoint_gain * residuals[moment][comp] * rec_lane for comp in range(3)],
             axis=1,
         )
-        high, middle, low = split3(scaled)
-        contract = (((0,), (0,)), ((), ()))
-        spreaded = sum(
-            lax.dot_general(
-                rec_rows, part, contract, preferred_element_type=jnp.float32
+        injected = sum(dot(rows_lanes, part) for part in split3(scaled))
+        for comp in range(3):
+            force[comp] = injected[:, comp * LANES : (comp + 1) * LANES].reshape(
+                5, 5, 8, LANES
             )
-            for part in (high, middle, low)
-        )
-        for comp in range(3):
-            clamped = spreaded[:, comp * LANES : (comp + 1) * LANES]
-            ev_load = clamped.reshape(5, 5, 8, LANES)
-            force[comp] = ev_load
 
         def beside(moment=moment):
+            add_kernels(moment, last_forward if moment == steps - 1 else None)
             if moment == steps - 1:
-                put_out(0, final_f_ref)
+                put_out(last_forward, final_f_ref)
+            if moment == 0:
+                send_kernels()
 
         run_step(
-            2,
+            index,
+            older,
             2 * steps - 1 - moment,
-            None,
-            moment,
+            astrain,
             lambda comp, a: force[comp, a],
             beside,
         )
-        swap(2)
-
-    both = jnp.concatenate(
-        [ksum[0].reshape(200, LANES), ksum[1].reshape(200, LANES)], axis=1
-    )
-    natural = move_left(rows_t_ref[...], both)
-    width = LANES // n_event
-    k_lam = natural[:, 0:LANES] * (-time_step * lam_ref[...])
-    k_mu = natural[:, LANES : 2 * LANES] * (-2.0 * time_step * mu_ref[...])
-    lane2 = lax.broadcasted_iota(jnp.int32, (125, LANES), 1)
-
-    def packed_for(target):
-        shift = lax.rem(LANES - width * target, LANES)
-        return jnp.where(
-            lane2 < width,
-            pltpu.roll(k_lam, shift, 1),
-            pltpu.roll(k_mu, lax.rem(shift + width, LANES), 1),
-        )
-
-    def event_copy(hop):
-        return pltpu.make_async_remote_copy(
-            src_ref=ev_s.at[hop - 1], dst_ref=ev_r.at[hop - 1],
-            send_sem=s_ev.at[hop - 1], recv_sem=r_ev.at[hop - 1],
-            device_id={"event": lax.rem(event + hop, n_event)},
-        )
-
-    for hop in range(1, n_event):
-        ev_s[hop - 1] = packed_for(lax.rem(event + hop, n_event))
-        event_copy(hop).start()
-    put_out(2, final_a_ref)
-    total = packed_for(event)
+        index, older = older, index
+
+    put_out(index, final_a_ref)
+    mine = pl.ds(pl.multiple_of(width * event, width), width)
+    total = ev_s[:, mine]
     for hop in range(1, n_event):
         event_copy(hop).wait_recv()
         total = total + ev_r[hop - 1]
-    out_ref[0] = total[:, 0:width]
-    out_ref[1] = total[:, width : 2 * width]
+    out_ref[...] = total
 
     @pl.when(has_up)
     def _():
@@ -596,27 +667,42 @@
     assert forward_now.shape[1:] == (3, 8, 8, 128)
     assert lame_mu.shape == (125, 128)
     steps = source_force.shape[1]
-    source = jnp.concatenate([source_element, source_offset[0]])
     field = forward_now.shape
     vmem = pl.BlockSpec(memory_space=pltpu.VMEM)
+    hbm = pl.BlockSpec(memory_space=pltpu.HBM)
     smem = pl.BlockSpec(memory_space=pltpu.SMEM)
     f32 = jnp.float32
     elem = (5, 5, 8, LANES)
     slots = 2 * steps + 1
-    return pl.pallas_call(
+    copied = (
+        forward_now,
+        forward_before,
+        adjoint_now,
+        adjoint_after,
+        mass_density,
+        lame_lambda,
+        lame_mu,
+        receiver_element,
+        receiver_offset.transpose(2, 0, 1),
+        receiver_data.transpose(1, 3, 0, 2),
+    ) + constants()[:-1]
+    final_f, final_a, kernels = pl.pallas_call(
         functools.partial(kernel, n_mesh, n_event, steps),
         out_shape=(
             jax.ShapeDtypeStruct(field, f32),
             jax.ShapeDtypeStruct(field, f32),
-            jax.ShapeDtypeStruct((2, 125, LANES // n_event), f32),
+            jax.ShapeDtypeStruct((2, LANES // n_event, 125), f32),
         ),
-        in_specs=[vmem] * 7 + [smem, smem] + [vmem] * 3 + [vmem] * 6 + [smem],
+        in_specs=[hbm] * 15 + [smem] * 4,
         out_specs=(vmem, vmem, vmem),
-        scratch_shapes=[
+        scratch_shapes=[pltpu.VMEM(value.shape, value.dtype) for value in copied]
+        + [
+            pltpu.SemaphoreType.DMA((len(copied),)),
             pltpu.VMEM((4, 3) + elem, f32),
             pltpu.VMEM((6,) + elem, f32),
             pltpu.VMEM((3,) + elem, f32),
             pltpu.VMEM((steps, 5, 6, 5, 8, LANES), f32),
+            pltpu.VMEM((5, 6, 5, 8, LANES), f32),
             pltpu.VMEM((2,) + elem, f32),
             pltpu.VMEM(elem, f32),
             pltpu.VMEM(elem, f32),
@@ -627,8 +713,8 @@
             pltpu.VMEM((slots, 3, 2, 8, LANES), f32),
             pltpu.VMEM((slots, 3, 2, 8, LANES), f32),
             pltpu.VMEM((slots, 3, 2, 8, LANES), f32),
-            pltpu.VMEM((max(1, n_event - 1), 125, LANES), f32),
-            pltpu.VMEM((max(1, n_event - 1), 125, LANES), f32),
+            pltpu.VMEM((2, LANES, 125), f32),
+            pltpu.VMEM((max(1, n_event - 1), 2, LANES // n_event, 125), f32),
             pltpu.SemaphoreType.DMA((slots + 1,)),
             pltpu.SemaphoreType.DMA((slots + 1,)),
             pltpu.SemaphoreType.DMA((slots,)),
@@ -637,23 +723,16 @@
             pltpu.SemaphoreType.DMA((max(1, n_event - 1),)),
         ],
         compiler_params=pltpu.CompilerParams(
-            collective_id=0, has_side_effects=True, vmem_limit_bytes=48 * 1024 * 1024
+            collective_id=0, has_side_effects=True, vmem_limit_bytes=60 * 1024 * 1024
         ),
     )(
-        forward_now,
-        forward_before,
-        adjoint_now,
-        adjoint_after,
-        mass_density,
-        lame_lambda,
-        lame_mu,
-        source,
-        source_force.reshape(-1),
-        receiver_element.reshape(-1, 1),
-        receiver_offset,
-        receiver_data,
-        *constants(),
+        *copied,
+        source_element,
+        source_offset,
+        source_force.transpose(1, 0, 2),
+        constants()[-1],
     )
+    return (final_f, final_a, kernels.transpose(0, 2, 1))
 
 
 def solution(mesh):

time: 58.7 us -> 41.5 us (0.71)
  local copies, waits for them, and re-layouts: 15 us -> 3.07 us
  Pallas kernels: 40.2 us -> 36.9 us
  other arithmetic: 1.43 us -> 0 us
    unnamed x32 -> x7, local copies, waits for them, and re-layouts: 13.4 us -> 3.07 us
    pallas_call x1, Pallas kernels: 40.2 us -> 36.9 us  [on_device(): pl.pallas_call(functools.partial(kernel, n_mesh, n_event, steps), out_sha...]
    reshape x2 -> x0, local copies, waits for them, and re-layouts: 0.82 us -> none  [the longest x1 0.74 us: on_device(): receiver_element.reshape(-1, 1)]
    concatenate x1 -> x0, other arithmetic: 0.73 us -> none  [on_device(): source = jnp.concatenate([source_element, source_offset[0]])]
    pallas_call x1 -> x0, local copies, waits for them, and re-layouts: 0.72 us -> none  [on_device(): pl.pallas_call(functools.partial(kernel, n_mesh, n_event, steps), out_sha...]
    unnamed x1 -> x0, other arithmetic: 0.7 us -> none
where the time goes in v1:
time: 41.5 us; the launch traced here: 41.3 us
  Pallas kernels  36.9 us (89%)
  local copies, waits for them, and re-layouts  3.07 us (7%)
  between operations  1.3 us (3%)
    pallas_call x1, Pallas kernels, on_device(): pl.pallas_call(functools.partial(kernel, n_mesh, n_event, steps), out_sha...  36.9 us
    unnamed x7, local copies, waits for them, and re-layouts  3.07 us

profile of v1, /device:TPU:24, one launch (start us, length us, event | category | flops | bytes accessed | tf_op | source)
XLA Modules:
  0.0 41.3 jit_solution(14233153741681498322)
XLA Ops:
  1.3 36.9 %shard_map.202 = (f32[1,3,8,8,128]{4,3,2,1,0:T(8,128)}, f32[1,3,8,8,128]{4,3,2,1,0:T(8,128)}, f32[2,64,125]{2,1,0:T(8,128)}) custom-call(f32[1,3,8,8,128]{4,3,2,1,0:T(8,128)} %now_hbm.1, f32[1,3,8,8,128]{4,3,2,1,0:T(8,128)} %before_hbm.1, f32[1,3,8,8,128]{4,3,2,1,0:T(8,128)} %adj_hbm.1, f32[1,3,8,8,128]{4,3,2,1,0:T(8,128)} %after_hbm.1, f32[125,128]{1,0:T(8,128)} %rho_hbm.1, ...), custom_call_target="tpu_custom_call" | custom-call | tf_op jit(solution)/shard_map/pallas_call | solution.py:689
  38.2 0.0 copy-start
  38.2 1.6 %copy.26 = f32[1,3,8,8,128]{4,3,2,1,0:T(8,128)} copy(f32[1,3,8,8,128]{4,3,2,1,0:T(8,128)} %get-tuple-element.12) | data formatting | bytes 196608
  39.8 0.0 copy-done
  39.8 0.0 copy-start.1
  39.8 0.6 %copy.27 = f32[1,3,8,8,128]{4,3,2,1,0:T(8,128)} copy(f32[1,3,8,8,128]{4,3,2,1,0:T(8,128)S(1)} %copy-done) | data formatting | bytes 196608
  40.4 0.2 copy-done.1
  40.7 0.6 %copy.28 = f32[2,125,64]{1,2,0:T(8,128)} copy(f32[2,125,64]{1,2,0:T(8,128)S(1)} %bitcast.4) | data formatting | bytes 128000
Async XLA Ops:
  38.2 1.6 %copy-start = (f32[1,3,8,8,128]{4,3,2,1,0:T(8,128)S(1)}, f32[1,3,8,8,128]{4,3,2,1,0:T(8,128)}, u32[]{:S(2)}) copy-start(f32[1,3,8,8,128]{4,3,2,1,0:T(8,128)} %get-tuple-element.13) | copy-start | bytes 294916
  39.8 0.9 %copy-start.1 = (f32[2,64,125]{2,1,0:T(8,128)S(1)}, f32[2,64,125]{2,1,0:T(8,128)}, u32[]{:S(2)}) copy-start(f32[2,64,125]{2,1,0:T(8,128)} %get-tuple-element.8) | copy-start | bytes 192004

commit v2 on v1

--- a/solution.py
+++ b/solution.py
@@ -53,7 +53,6 @@
         for b in range(5):
             dy[0, k, b, :] = DERIV[b, k]
             dy[1, k, b, :] = DERIV[k, b]
-    dz = np.stack([DERIV, DERIV.T]).reshape(-1).astype(np.float32)
     bf = jnp.bfloat16
     return (
         jnp.asarray(spread, bf),
@@ -61,7 +60,6 @@
         jnp.asarray(rows, bf),
         jnp.asarray(cube),
         jnp.asarray(dy),
-        jnp.asarray(dz),
     )
 
 
@@ -136,6 +134,11 @@
         lane_iota(4) % 64 < 32, roll_lane(swapped, -32), roll_lane(swapped, 32)
     )
     return value + pick(sub_iota(4) % 4 == 0, other, jnp.zeros_like(other))
+
+
+def each(first, last, body):
+    for a in range(first, last):
+        body(a, 0)
 
 
 def kernel(
@@ -160,7 +163,6 @@
     elem_ref,
     off_ref,
     force_ref,
-    dz_ref,
     final_f_ref,
     final_a_ref,
     out_ref,
@@ -426,8 +428,9 @@
             row_k = jnp.broadcast_to(plane[:, :, k : k + 1], plane.shape)
             term = dy_ref[0, k] * row_k
             gy = term if gy is None else gy + term
-            term = dz_ref[a * 5 + k] * fields[index, :, k]
-            gz = term if gz is None else gz + term
+            if DERIV[a, k] != 0.0:
+                term = float(DERIV[a, k]) * fields[index, :, k]
+                gz = term if gz is None else gz + term
         return (
             gx[0],
             gy[1],
@@ -458,7 +461,7 @@
                 ksum[1, a] = ksum[1, a] + mu_part
             return carry
 
-        lax.fori_loop(0, 5, body, 0)
+        each(0, 5, body)
 
     def run_step(index, older, slot, keep_strain, load, beside):
         def stress_body(a, carry):
@@ -474,7 +477,7 @@
                     keep_strain[a, i] = strain[i]
             return carry
 
-        lax.fori_loop(0, 5, stress_body, 0)
+        each(0, 5, stress_body)
 
         def force_body(a, carry):
             along = ((0, 3, 4), (3, 1, 5), (4, 5, 2))
@@ -494,12 +497,13 @@
                 for q in range(5):
                     row_q = jnp.broadcast_to(sy[:, q : q + 1], sy.shape)
                     total = total + dy_ref[1, q] * row_q
-                    total = total + dz_ref[25 + a * 5 + q] * stress[along[comp][2], q]
+                    if DERIV[q, a] != 0.0:
+                        total = total + float(DERIV[q, a]) * stress[along[comp][2], q]
                 force[comp, a] = total - load(comp, a)
             force[:, a] = assemble_xy(force[:, a])
             return carry
 
-        lax.fori_loop(0, 5, force_body, 0)
+        each(0, 5, force_body)
         send_faces(force[:, 0], force[:, 4], slot)
         beside()
 
@@ -509,7 +513,7 @@
             ) - minv[a] * force[:, a]
             return carry
 
-        lax.fori_loop(1, 4, inner, 0)
+        each(1, 4, inner)
         top, bottom = finish_faces(force[:, 0], force[:, 4], slot)
         for a, plane in ((0, top), (4, bottom)):
             fields[older, :, a] = (
@@ -685,7 +689,7 @@
         receiver_element,
         receiver_offset.transpose(2, 0, 1),
         receiver_data.transpose(1, 3, 0, 2),
-    ) + constants()[:-1]
+    ) + constants()
     final_f, final_a, kernels = pl.pallas_call(
         functools.partial(kernel, n_mesh, n_event, steps),
         out_shape=(
@@ -693,7 +697,7 @@
             jax.ShapeDtypeStruct(field, f32),
             jax.ShapeDtypeStruct((2, LANES // n_event, 125), f32),
         ),
-        in_specs=[hbm] * 15 + [smem] * 4,
+        in_specs=[hbm] * 15 + [smem] * 3,
         out_specs=(vmem, vmem, vmem),
         scratch_shapes=[pltpu.VMEM(value.shape, value.dtype) for value in copied]
         + [
@@ -730,7 +734,6 @@
         source_element,
         source_offset,
         source_force.transpose(1, 0, 2),
-        constants()[-1],
     )
     return (final_f, final_a, kernels.transpose(0, 2, 1))
 

time: 41.5 us -> 35.8 us (0.86)
  Pallas kernels: 36.9 us -> 31.1 us
    pallas_call x1, Pallas kernels: 36.9 us -> 31.1 us  [on_device(): pl.pallas_call(functools.partial(kernel, n_mesh, n_event, steps), out_sha...]
where the time goes in v2:
time: 35.8 us; the launch traced here: 35.4 us
  Pallas kernels  31.1 us (87%)
  local copies, waits for them, and re-layouts  3.07 us (9%)
  between operations  1.3 us (4%)
    pallas_call x1, Pallas kernels, on_device(): pl.pallas_call(functools.partial(kernel, n_mesh, n_event, steps), out_sha...  31.1 us
    unnamed x7, local copies, waits for them, and re-layouts  3.07 us

profile of v2, /device:TPU:24, one launch (start us, length us, event | category | flops | bytes accessed | tf_op | source)
XLA Modules:
  0.0 35.4 jit_solution(16773223120014768318)
XLA Ops:
  1.3 31.1 %shard_map.193 = (f32[1,3,8,8,128]{4,3,2,1,0:T(8,128)}, f32[1,3,8,8,128]{4,3,2,1,0:T(8,128)}, f32[2,64,125]{2,1,0:T(8,128)}) custom-call(f32[1,3,8,8,128]{4,3,2,1,0:T(8,128)} %now_hbm.1, f32[1,3,8,8,128]{4,3,2,1,0:T(8,128)} %before_hbm.1, f32[1,3,8,8,128]{4,3,2,1,0:T(8,128)} %adj_hbm.1, f32[1,3,8,8,128]{4,3,2,1,0:T(8,128)} %after_hbm.1, f32[125,128]{1,0:T(8,128)} %rho_hbm.1, ...), custom_call_target="tpu_custom_call" | custom-call | tf_op jit(solution)/shard_map/pallas_call | solution.py:693
  32.4 0.0 copy-start
  32.4 1.6 %copy.25 = f32[1,3,8,8,128]{4,3,2,1,0:T(8,128)} copy(f32[1,3,8,8,128]{4,3,2,1,0:T(8,128)} %get-tuple-element.12) | data formatting | bytes 196608
  33.9 0.0 copy-done
  33.9 0.0 copy-start.1
  33.9 0.6 %copy.26 = f32[1,3,8,8,128]{4,3,2,1,0:T(8,128)} copy(f32[1,3,8,8,128]{4,3,2,1,0:T(8,128)S(1)} %copy-done) | data formatting | bytes 196608
  34.6 0.2 copy-done.1
  34.8 0.6 %copy.27 = f32[2,125,64]{1,2,0:T(8,128)} copy(f32[2,125,64]{1,2,0:T(8,128)S(1)} %bitcast.4) | data formatting | bytes 128000
Async XLA Ops:
  32.4 1.6 %copy-start = (f32[1,3,8,8,128]{4,3,2,1,0:T(8,128)S(1)}, f32[1,3,8,8,128]{4,3,2,1,0:T(8,128)}, u32[]{:S(2)}) copy-start(f32[1,3,8,8,128]{4,3,2,1,0:T(8,128)} %get-tuple-element.13) | copy-start | bytes 294916
  33.9 0.9 %copy-start.1 = (f32[2,64,125]{2,1,0:T(8,128)S(1)}, f32[2,64,125]{2,1,0:T(8,128)}, u32[]{:S(2)}) copy-start(f32[2,64,125]{2,1,0:T(8,128)} %get-tuple-element.8) | copy-start | bytes 192004

commit v3 on v2

--- a/solution.py
+++ b/solution.py
@@ -503,7 +503,8 @@
             force[:, a] = assemble_xy(force[:, a])
             return carry
 
-        each(0, 5, force_body)
+        force_body(0, 0)
+        force_body(4, 0)
         send_faces(force[:, 0], force[:, 4], slot)
         beside()
 
@@ -513,6 +514,7 @@
             ) - minv[a] * force[:, a]
             return carry
 
+        each(1, 4, force_body)
         each(1, 4, inner)
         top, bottom = finish_faces(force[:, 0], force[:, 4], slot)
         for a, plane in ((0, top), (4, bottom)):
@@ -613,7 +615,7 @@
 
         def beside(moment=moment):
             add_kernels(moment, last_forward if moment == steps - 1 else None)
-            if moment == steps - 1:
+            if moment == max(steps - 2, 0):
                 put_out(last_forward, final_f_ref)
             if moment == 0:
                 send_kernels()

time: 35.8 us -> 34.3 us (0.958)
  Pallas kernels: 31.1 us -> 29.6 us
    pallas_call x1, Pallas kernels: 31.1 us -> 29.6 us  [on_device(): pl.pallas_call(functools.partial(kernel, n_mesh, n_event, steps), out_sha...]
where the time goes in v3:
time: 34.3 us; the launch traced here: 34 us
  Pallas kernels  29.6 us (86%)
  local copies, waits for them, and re-layouts  3.07 us (9%)
  between operations  1.3 us (4%)
    pallas_call x1, Pallas kernels, on_device(): pl.pallas_call(functools.partial(kernel, n_mesh, n_event, steps), out_sha...  29.6 us
    unnamed x7, local copies, waits for them, and re-layouts  3.07 us

profile of v3, /device:TPU:24, one launch (start us, length us, event | category | flops | bytes accessed | tf_op | source)
XLA Modules:
  0.0 34.0 jit_solution(11966833031638281400)
XLA Ops:
  1.3 29.6 %shard_map.193 = (f32[1,3,8,8,128]{4,3,2,1,0:T(8,128)}, f32[1,3,8,8,128]{4,3,2,1,0:T(8,128)}, f32[2,64,125]{2,1,0:T(8,128)}) custom-call(f32[1,3,8,8,128]{4,3,2,1,0:T(8,128)} %now_hbm.1, f32[1,3,8,8,128]{4,3,2,1,0:T(8,128)} %before_hbm.1, f32[1,3,8,8,128]{4,3,2,1,0:T(8,128)} %adj_hbm.1, f32[1,3,8,8,128]{4,3,2,1,0:T(8,128)} %after_hbm.1, f32[125,128]{1,0:T(8,128)} %rho_hbm.1, ...), custom_call_target="tpu_custom_call" | custom-call | tf_op jit(solution)/shard_map/pallas_call | solution.py:695
  30.9 0.0 copy-start
  30.9 1.6 %copy.25 = f32[1,3,8,8,128]{4,3,2,1,0:T(8,128)} copy(f32[1,3,8,8,128]{4,3,2,1,0:T(8,128)} %get-tuple-element.12) | data formatting | bytes 196608
  32.5 0.0 copy-done
  32.5 0.0 copy-start.1
  32.5 0.6 %copy.26 = f32[1,3,8,8,128]{4,3,2,1,0:T(8,128)} copy(f32[1,3,8,8,128]{4,3,2,1,0:T(8,128)S(1)} %copy-done) | data formatting | bytes 196608
  33.2 0.2 copy-done.1
  33.4 0.6 %copy.27 = f32[2,125,64]{1,2,0:T(8,128)} copy(f32[2,125,64]{1,2,0:T(8,128)S(1)} %bitcast.4) | data formatting | bytes 128000
Async XLA Ops:
  30.9 1.6 %copy-start = (f32[1,3,8,8,128]{4,3,2,1,0:T(8,128)S(1)}, f32[1,3,8,8,128]{4,3,2,1,0:T(8,128)}, u32[]{:S(2)}) copy-start(f32[1,3,8,8,128]{4,3,2,1,0:T(8,128)} %get-tuple-element.13) | copy-start | bytes 294916
  32.5 0.9 %copy-start.1 = (f32[2,64,125]{2,1,0:T(8,128)S(1)}, f32[2,64,125]{2,1,0:T(8,128)}, u32[]{:S(2)}) copy-start(f32[2,64,125]{2,1,0:T(8,128)} %get-tuple-element.8) | copy-start | bytes 192004
